TPU v7x, 32 devices: a whole 2x2x4 slice. The times are simulated.
32 devices in a mesh: dp: 4 (over z), mp: 8 (over y, x, core).
Axes of the slice: x: 2, y: 2, z: 4, core: 2. Of those that a mesh axis runs over, the one named last changes fastest.
Arguments:
- behaviors: bfloat16 [32, 2048, 1024], P('dp', 'mp'), may hold values from -8 to 8
- candidates: bfloat16 [32, 2048, 128], P('dp', 'mp'), may hold values from -12 to 12
- lengths: int32 [32], P('dp'), may hold values from 128 to 1024
- bilinear: bfloat16 [2048, 2048], P('mp'), may hold values from -1 to 2
- norm_gain: float32 [2048], replicated, may hold values from 0.1 to 1.9
- w_gate: bfloat16 [2048, 8192], P('dp', 'mp'), may hold values from -0.125 to 0.125
- w_up: bfloat16 [2048, 8192], P('dp', 'mp'), may hold values from -0.125 to 0.125
- w_down: bfloat16 [8192, 2048], P('mp', 'dp'), may hold values from -0.0625 to 0.0625
Outputs:
- interest: bfloat16 [32, 2048, 128], P('dp', 'mp')
All inputs are finite; a program needn't handle non-finite values.
Results may differ from a plain program's by a relative error of at most 0.015.
Values may be sent and summed in bfloat16 or wider, within the bound.
No kernel may reach another device: no remote copies, remote signals or barrier semaphores. Data moves between devices by JAX's collectives and lax.ppermute only.
A program may use at most 64 MiB of HBM per device.

v0:
```python
import math
import jax
import jax.numpy as jnp
from jax import lax
from jax.sharding import PartitionSpec as P


def attention_weights(scores, live):
    masked = jnp.where(live, scores, -1e30)
    highest = jnp.max(masked, axis=-1, keepdims=True)
    expons = jnp.where(live, jnp.exp(masked - highest), 0.0)
    return (expons / jnp.sum(expons, axis=-1, keepdims=True)).astype(jnp.bfloat16)


def shards(behaviors, candidates, lengths, bilinear, norm_gain, w_gate, w_up, w_down):
    user_count, width_part, cand_count = candidates.shape
    feature_width = bilinear.shape[1]
    behavior_count = behaviors.shape[2]
    query_part = jnp.einsum(
        "ek,ukc->uec",
        bilinear,
        lax.all_gather(candidates, "mp", axis=1, tiled=True),
        preferred_element_type=jnp.float32,
    )
    query = query_part.astype(jnp.bfloat16)
    partial_value = jnp.einsum("ukc,ukl->ucl", query, behaviors, preferred_element_type=jnp.float32)
    scale = 1.0 / math.sqrt(feature_width)
    live = (
        lax.broadcasted_iota(jnp.int32, (user_count, 1, behavior_count), 2) < lengths[:, None, None]
    )
    share = lax.psum_scatter(partial_value, "mp", scatter_dimension=1, tiled=True)
    probs_share = attention_weights(share * scale, live)
    probs = lax.all_gather(probs_share, "mp", axis=1, tiled=True)
    pooled = jnp.einsum(
        "ucl,ukl->ukc", probs, behaviors, preferred_element_type=jnp.float32
    ).astype(jnp.bfloat16)
    whole = lax.all_gather(pooled, "mp", axis=1, tiled=True)
    values = whole.astype(jnp.float32)
    square_mean = jnp.mean(values * values, axis=1, keepdims=True)
    normed = (values * lax.rsqrt(square_mean + 1e-06) * norm_gain[None, :, None]).astype(
        jnp.bfloat16
    )
    gate = jnp.einsum(
        "ukc,kf->ucf",
        normed,
        lax.all_gather(w_gate, "dp", axis=0, tiled=True),
        preferred_element_type=jnp.float32,
    )
    upward = jnp.einsum(
        "ukc,kf->ucf",
        normed,
        lax.all_gather(w_up, "dp", axis=0, tiled=True),
        preferred_element_type=jnp.float32,
    )
    hidden = (jax.nn.silu(gate) * upward).astype(jnp.bfloat16)
    down_full = lax.all_gather(w_down, "dp", axis=1, tiled=True)
    result = lax.psum_scatter(
        jnp.einsum("ucf,fk->kuc", hidden, down_full, preferred_element_type=jnp.float32).astype(
            jnp.bfloat16
        ),
        "mp",
        scatter_dimension=0,
        tiled=True,
    ).astype(jnp.float32)
    return jnp.transpose(result, (1, 0, 2)).astype(jnp.bfloat16)


def solution(mesh):
    return jax.shard_map(
        shards,
        mesh=mesh,
        in_specs=(
            P("dp", "mp", None),
            P("dp", "mp", None),
            P("dp"),
            P("mp", None),
            P(),
            P("dp", "mp"),
            P("dp", "mp"),
            P("mp", "dp"),
        ),
        out_specs=P("dp", "mp", None),
        check_vma=False,
    )
```

profile of v0, /device:TPU:0, one launch (start us, length us, event | category | flops | bytes accessed | tf_op | source)
XLA Modules:
  0.0 498.7 jit_solution(1023455317639719504)
XLA Ops:
  6.5 0.0 copy-start
  6.5 0.0 all-gather.7.cloned.1.call-start
  6.5 0.7 all-gather.7.cloned.1.call-update
  7.3 0.0 reduce-scatter.3.cloned.1.call-start
  7.3 41.3 %all-gather.7.cloned.1.call-done = bf16[8,2048,128]{2,1,0:T(8,128)(2,1)} async-done(((bf16[8,256,128]{2,1,0:T(8,128)(2,1)}), bf16[8,2048,128]{2,1,0:T(8,128)(2,1)}) %all-gather.7.cloned.1.call-update) | async-done | bytes 4194320 | tf_op jit(solution)/shard_map/all_gather | solution.py:22
  48.6 0.0 copy-done
  48.6 8.2 %fusion.24 = f32[8,128,1024]{2,1,0:T(8,128)} fusion(bf16[8,256,1024]{2,1,0:T(8,128)(2,1)} %param.8, bf16[8,2048,128]{2,1,0:T(8,128)(2,1)} %all-gather.7.cloned.1.call-done, bf16[256,2048]{1,0:T(8,128)(2,1)S(1)} %copy-done), kind=kOutput, calls=%fused_computation.18 | convolution fusion | flops 1610874880 | bytes 13631488 | tf_op jit(solution)/shard_map/ukc,ukl->ucl/dot_general | solution.py:26
  56.7 0.0 copy-start.1
  56.7 0.0 reduce-scatter.3.cloned.1.call-update
  56.8 0.0 all-gather.9.cloned.1.call-start
  56.8 0.6 copy-done.1
  57.4 0.1 iota_compare_fusion
  57.5 50.5 %reduce-scatter.3.cloned.1.call-done = f32[8,16,1024]{2,1,0:T(8,128)} async-done(((f32[8,128,1024]{2,1,0:T(8,128)}), f32[8,16,1024]{2,1,0:T(8,128)}) %reduce-scatter.3.cloned.1.call-update) | async-done | bytes 524304 | tf_op jit(solution)/shard_map/reduce_scatter | solution.py:31
  108.0 1.7 fusion.37
  109.7 0.8 divide_convert_fusion
  110.5 0.0 all-gather.9.cloned.1.call-update
  110.6 0.0 all-gather.11.cloned.1.call-start
  110.6 27.9 %all-gather.9.cloned.1.call-done = bf16[8,128,1024]{2,1,0:T(8,128)(2,1)} async-done(((bf16[8,16,1024]{2,1,0:T(8,128)(2,1)}), bf16[8,128,1024]{2,1,0:T(8,128)(2,1)}) %all-gather.9.cloned.1.call-update) | async-done | bytes 2097168 | tf_op jit(solution)/shard_map/all_gather | solution.py:33
  138.5 5.2 %fusion.27 = bf16[8,256,128]{1,2,0:T(8,128)(2,1)} fusion(bf16[8,128,1024]{2,1,0:T(8,128)(2,1)} %all-gather.9.cloned.1.call-done, bf16[8,256,1024]{2,1,0:T(8,128)(2,1)} %param.8), kind=kOutput, calls=%fused_computation.21 | convolution fusion | flops 537133056 | bytes 6815744 | tf_op jit(solution)/shard_map/ucl,ukl->ukc/dot_general | solution.py:34
  143.7 0.0 copy-start.2
  143.7 0.0 all-gather.11.cloned.1.call-update
  143.7 0.0 all-gather.13.cloned.1.call-start
  143.7 0.5 all-gather.13.cloned.1.call-update
  144.3 0.0 all-gather.15.cloned.1.call-start
  144.3 0.5 all-gather.15.cloned.1.call-update
  144.8 0.0 all-gather.17.cloned.1.call-start
  144.9 0.7 all-gather.17.cloned.1.call-update
  145.6 0.2 reduce-scatter.5.cloned.1.call-start
  145.8 35.4 %all-gather.11.cloned.1.call-done = bf16[8,2048,128]{1,2,0:T(8,128)(2,1)} async-done(((bf16[8,256,128]{1,2,0:T(8,128)(2,1)}), bf16[8,2048,128]{1,2,0:T(8,128)(2,1)}) %all-gather.11.cloned.1.call-update) | async-done | bytes 4194320 | tf_op jit(solution)/shard_map/all_gather | solution.py:37
  181.2 3.1 fusion.1
  184.3 79.1 %all-gather.13.cloned.1.call-done = bf16[2048,1024]{1,0:T(8,128)(2,1)} async-done(((bf16[512,1024]{1,0:T(8,128)(2,1)}), bf16[2048,1024]{1,0:T(8,128)(2,1)}) %all-gather.13.cloned.1.call-update) | async-done | bytes 4194320 | tf_op jit(solution)/shard_map/all_gather | solution.py:46
  263.4 0.0 copy-done.2
  263.4 9.9 %fusion.8 = f32[8,128,1024]{2,1,0:T(8,128)} fusion(bf16[2048,1024]{1,0:T(8,128)(2,1)} %all-gather.13.cloned.1.call-done, bf16[8,2048,128]{1,2,0:T(8,128)(2,1)} %all-gather.11.cloned.1.call-done, f32[2048]{0:T(1024)S(1)} %copy-done.2, f32[8,128]{1,0:T(8,128)S(1)} %add_rsqrt_fusion), kind=kOutput, calls=%fused_computation.10 | convolution fusion | flops 4303355904 | bytes 12595200 | tf_op jit(solution)/shard_map/ukc,kf->ucf/dot_general | solution.py:43
  273.3 70.7 %all-gather.15.cloned.1.call-done = bf16[2048,1024]{1,0:T(8,128)(2,1)} async-done(((bf16[512,1024]{1,0:T(8,128)(2,1)}), bf16[2048,1024]{1,0:T(8,128)(2,1)}) %all-gather.15.cloned.1.call-update) | async-done | bytes 4194320 | tf_op jit(solution)/shard_map/all_gather | solution.py:52
  344.0 80.8 %all-gather.17.cloned.1.call-done = bf16[1024,2048]{1,0:T(8,128)(2,1)} async-done(((bf16[1024,512]{1,0:T(8,128)(2,1)}), bf16[1024,2048]{1,0:T(8,128)(2,1)}) %all-gather.17.cloned.1.call-update) | async-done | bytes 4194320 | tf_op jit(solution)/shard_map/all_gather | solution.py:56
  424.9 15.2 %convert_bitcast_fusion = bf16[2048,8,128]{0,2,1:T(8,128)(2,1)} fusion(bf16[1024,2048]{1,0:T(8,128)(2,1)} %all-gather.17.cloned.1.call-done, f32[8,128,1024]{2,1,0:T(8,128)} %fusion.8, bf16[2048,1024]{1,0:T(8,128)(2,1)} %all-gather.15.cloned.1.call-done, bf16[8,2048,128]{1,2,0:T(8,128)(2,1)} %all-gather.11.cloned.1.call-done, f32[2048]{0:T(1024)S(1)} %copy-done.2, ...), kind=kOutput, calls=%fused_computation.12 | convolution fusion | flops 8606711808 | bytes 20983808 | tf_op jit(solution)/shard_map/ucf,fk->kuc/dot_general | solution.py:58
  440.1 0.0 reduce-scatter.5.cloned.1.call-update
  440.1 49.7 %reduce-scatter.5.cloned.1.call-done = bf16[256,8,128]{0,2,1:T(8,128)(2,1)} async-done(((bf16[2048,8,128]{0,2,1:T(8,128)(2,1)}), bf16[256,8,128]{0,2,1:T(8,128)(2,1)}) %reduce-scatter.5.cloned.1.call-update) | async-done | bytes 524304 | tf_op jit(solution)/shard_map/reduce_scatter | solution.py:57
  489.8 2.0 copy.9
  (1 shorter events, 0.0 us)
Async XLA Ops:
  6.5 42.0 %copy-start = (bf16[256,2048]{1,0:T(8,128)(2,1)S(1)}, bf16[256,2048]{1,0:T(8,128)(2,1)}, u32[]{:S(2)}) copy-start(bf16[256,2048]{1,0:T(8,128)(2,1)} %param.11) | copy-start | bytes 3145732
  6.5 42.0 %all-gather.7.cloned.1.call-start = ((), (), s32[]{:S(2)}) async-start(), calls=%async_computation.2 | async-start | bytes 4718592 | tf_op jit(solution)/shard_map/all_gather | solution.py:22
  7.3 100.8 %reduce-scatter.3.cloned.1.call-start = ((), (), s32[]{:S(2)}) async-start(), calls=%async_computation.3 | async-start | bytes 4718592 | tf_op jit(solution)/shard_map/reduce_scatter | solution.py:31
  56.7 0.7 copy-start.1
  56.8 81.7 %all-gather.9.cloned.1.call-start = ((), (), s32[]{:S(2)}) async-start(), calls=%async_computation.4 | async-start | bytes 2359296 | tf_op jit(solution)/shard_map/all_gather | solution.py:33
  110.6 70.6 %all-gather.11.cloned.1.call-start = ((), (), s32[]{:S(2)}) async-start(), calls=%async_computation.5 | async-start | bytes 4718592 | tf_op jit(solution)/shard_map/all_gather | solution.py:37
  143.7 119.7 %copy-start.2 = (f32[2048]{0:T(1024)S(1)}, f32[2048]{0:T(1024)}, u32[]{:S(2)}) copy-start(f32[2048]{0:T(1024)} %param.12) | copy-start | bytes 24580
  143.7 119.7 %all-gather.13.cloned.1.call-start = ((), (), s32[]{:S(2)}) async-start(), calls=%async_computation.6 | async-start | bytes 5242880 | tf_op jit(solution)/shard_map/all_gather | solution.py:46
  144.3 199.8 %all-gather.15.cloned.1.call-start = ((), (), s32[]{:S(2)}) async-start(), calls=%async_computation.7 | async-start | bytes 5242880 | tf_op jit(solution)/shard_map/all_gather | solution.py:52
  144.8 280.0 %all-gather.17.cloned.1.call-start = ((), (), s32[]{:S(2)}) async-start(), calls=%async_computation.8 | async-start | bytes 5242880 | tf_op jit(solution)/shard_map/all_gather | solution.py:56
  145.6 344.2 %reduce-scatter.5.cloned.1.call-start = ((), (), s32[]{:S(2)}) async-start(), calls=%async_computation.9 | async-start | bytes 4718592 | tf_op jit(solution)/shard_map/reduce_scatter | solution.py:57
Sparse Core Ops, SparseCore 0:
  9.2 39.2 all-gather.6
  56.9 51.0 reduce-scatter.2
  110.7 27.7 all-gather.8
  143.8 37.3 all-gather.10
  182.6 80.7 all-gather.12
  264.8 79.2 all-gather.14
  345.6 79.2 all-gather.16
  440.2 49.5 reduce-scatter.4
where the time goes:
time: 499 us
  waiting for transfers between devices  438 us (88%)
  matrix products  38.4 us (8%)
  between operations  13.5 us (3%)
  other arithmetic  5.68 us (1%)
    all_gather x1, waiting for transfers between devices, shards(): down_full = lax.all_gather(w_down, 'dp', axis=1, tiled=True)  80.8 us
    all_gather x1, waiting for transfers between devices, shards(): lax.all_gather(w_gate, 'dp', axis=0, tiled=True)  79.1 us
    all_gather x1, waiting for transfers between devices, shards(): lax.all_gather(w_up, 'dp', axis=0, tiled=True)  70.7 us
    reduce_scatter x1, waiting for transfers between devices, shards(): lax.psum_scatter(partial_value, 'mp', scatter_dimension=1, tiled=True)  50.5 us
    reduce_scatter x1, waiting for transfers between devices, shards(): lax.psum_scatter(jnp.einsum('ucf,fk->kuc', hidden, down_full, preferred_e...  49.7 us
    all_gather x1, waiting for transfers between devices, shards(): lax.all_gather(candidates, 'mp', axis=1, tiled=True)  41.3 us
    all_gather x1, waiting for transfers between devices, shards(): whole = lax.all_gather(pooled, 'mp', axis=1, tiled=True)  35.4 us
    all_gather x1, waiting for transfers between devices, shards(): probs = lax.all_gather(probs_share, 'mp', axis=1, tiled=True)  27.9 us
  transfers between devices with their start and end apart: 8, of which 8 were waited for; matrix products, arithmetic and copies ran while one was open for 3% of the time, Pallas kernels for 0%

commit v1 on v0

--- a/solution.py
+++ b/solution.py
@@ -3,6 +3,30 @@
 import jax.numpy as jnp
 from jax import lax
 from jax.sharding import PartitionSpec as P
+
+
+def ring_apply(shard, axis, dim, work, out_dim):
+    size, position, rows = (lax.axis_size(axis), lax.axis_index(axis), shard.shape[dim])
+    right = [(i, (i + 1) % size) for i in range(size)]
+    backward = [(b, a) for a, b in right]
+    lower, upper = (lax.ppermute(shard, axis, right), lax.ppermute(shard, axis, backward))
+    made = work(shard, position * rows)
+    length = made.shape[out_dim]
+    out = jnp.zeros((*made.shape[:out_dim], size * length, *made.shape[out_dim + 1 :]), made.dtype)
+
+    def put(out, made, holder):
+        return lax.dynamic_update_slice_in_dim(out, made, holder * length, axis=out_dim)
+
+    out = put(out, made, position)
+    for step in range(1, size // 2 + 1):
+        below, above = ((position - step) % size, (position + step) % size)
+        carried = (lower, upper)
+        if step < size // 2:
+            lower, upper = (lax.ppermute(lower, axis, right), lax.ppermute(upper, axis, backward))
+        out = put(out, work(carried[0], below * rows), below)
+        if 2 * step < size:
+            out = put(out, work(carried[1], above * rows), above)
+    return out
 
 
 def attention_weights(scores, live):
@@ -53,11 +77,16 @@
         preferred_element_type=jnp.float32,
     )
     hidden = (jax.nn.silu(gate) * upward).astype(jnp.bfloat16)
-    down_full = lax.all_gather(w_down, "dp", axis=1, tiled=True)
     result = lax.psum_scatter(
-        jnp.einsum("ucf,fk->kuc", hidden, down_full, preferred_element_type=jnp.float32).astype(
-            jnp.bfloat16
-        ),
+        ring_apply(
+            w_down,
+            "dp",
+            1,
+            lambda shard, offset: jnp.einsum(
+                "ucf,fk->kuc", hidden, shard, preferred_element_type=jnp.float32
+            ),
+            0,
+        ).astype(jnp.bfloat16),
         "mp",
         scatter_dimension=0,
         tiled=True,

time: 499 us -> 462 us (0.926)
  waiting for transfers between devices: 438 us -> 375 us
  local copies, waits for them, and re-layouts: 2.63 us -> 16.1 us
  matrix products: 38.4 us -> 47.6 us
    all_gather x1 -> x0, waiting for transfers between devices: 80.8 us -> none  [shards(): down_full = lax.all_gather(w_down, 'dp', axis=1, tiled=True)]
    all_gather x1, waiting for transfers between devices: 70.7 us -> 101 us  [shards(): lax.all_gather(w_up, 'dp', axis=0, tiled=True)]
    all_gather x1, waiting for transfers between devices: 35.4 us -> 8.03 us  [shards(): whole = lax.all_gather(pooled, 'mp', axis=1, tiled=True)]
    ppermute x0 -> x3, waiting for transfers between devices: none -> 24.4 us  [the longest x1 24.4 us: ring_apply(): lax.ppermute(shard, axis, right)]
    dot_general x1 -> x5, matrix products: 15.2 us -> 24.6 us  [the longest x4 14.7 us: shards(): jnp.einsum('ucf,fk->kuc', hidden, shard, preferred_element_type=jnp.float32)]
    all_gather x1, waiting for transfers between devices: 79.1 us -> 70.3 us  [shards(): lax.all_gather(w_gate, 'dp', axis=0, tiled=True)]
    dot_general x0 -> x4, local copies, waits for them, and re-layouts: none -> 7.04 us  [shards(): jnp.einsum('ucf,fk->kuc', hidden, shard, preferred_element_type=jnp.float32)]
  transfers between devices with their start and end apart: 8 -> 10, of which waited for: 8 -> 8; matrix products, arithmetic and copies ran while one was open for 3% -> 8% of each run, Pallas kernels for 0% -> 0%
where the time goes in v1:
time: 462 us
  waiting for transfers between devices  375 us (81%)
  matrix products  47.6 us (10%)
  local copies, waits for them, and re-layouts  16.1 us (3%)
  between operations  13.6 us (3%)
  other arithmetic  5.65 us (1%)
    all_gather x1, waiting for transfers between devices, shards(): lax.all_gather(w_up, 'dp', axis=0, tiled=True)  101 us
    all_gather x1, waiting for transfers between devices, shards(): lax.all_gather(w_gate, 'dp', axis=0, tiled=True)  70.3 us
    reduce_scatter x1, waiting for transfers between devices, shards(): lax.psum_scatter(partial_value, 'mp', scatter_dimension=1, tiled=True)  50.5 us
    reduce_scatter x1, waiting for transfers between devices, shards(): lax.psum_scatter(ring_apply(w_down, 'dp', 1, lambda shard, offset: jnp.ei...  49.7 us
    all_gather x1, waiting for transfers between devices, shards(): lax.all_gather(candidates, 'mp', axis=1, tiled=True)  41.3 us
    all_gather x1, waiting for transfers between devices, shards(): probs = lax.all_gather(probs_share, 'mp', axis=1, tiled=True)  27.9 us
    ppermute x1, waiting for transfers between devices, ring_apply(): lax.ppermute(shard, axis, right)  24.4 us
    dot_general x4, matrix products, shards(): jnp.einsum('ucf,fk->kuc', hidden, shard, preferred_element_type=jnp.float32)  14.7 us
  transfers between devices with their start and end apart: 10, of which 8 were waited for; matrix products, arithmetic and copies ran while one was open for 8% of the time, Pallas kernels for 0%

profile of v1, /device:TPU:0, one launch (start us, length us, event | category | flops | bytes accessed | tf_op | source)
XLA Modules:
  0.0 461.9 jit_solution(16532105492516784224)
XLA Ops:
  6.5 0.7 all-gather.6.cloned.1.call-update
  7.3 0.0 reduce-scatter.3.cloned.1.call-start
  7.3 41.3 %all-gather.6.cloned.1.call-done = bf16[8,2048,128]{2,1,0:T(8,128)(2,1)} async-done(((bf16[8,256,128]{2,1,0:T(8,128)(2,1)}), bf16[8,2048,128]{2,1,0:T(8,128)(2,1)}) %all-gather.6.cloned.1.call-update) | async-done | bytes 4194320 | tf_op jit(solution)/shard_map/all_gather | solution.py:46
  48.6 8.2 %fusion.15 = f32[8,128,1024]{2,1,0:T(8,128)} fusion(bf16[8,256,1024]{2,1,0:T(8,128)(2,1)} %param.8, bf16[8,2048,128]{2,1,0:T(8,128)(2,1)} %all-gather.6.cloned.1.call-done, bf16[256,2048]{1,0:T(8,128)(2,1)S(1)} %copy-done), kind=kOutput, calls=%fused_computation.18 | convolution fusion | flops 1610874880 | bytes 13631488 | tf_op jit(solution)/shard_map/ukc,ukl->ucl/dot_general | solution.py:50
  56.8 0.0 reduce-scatter.3.cloned.1.call-update
  56.8 0.0 all-gather.8.cloned.1.call-start
  56.8 0.6 copy-done.3
  57.4 0.1 iota_compare_fusion
  57.5 50.5 %reduce-scatter.3.cloned.1.call-done = f32[8,16,1024]{2,1,0:T(8,128)} async-done(((f32[8,128,1024]{2,1,0:T(8,128)}), f32[8,16,1024]{2,1,0:T(8,128)}) %reduce-scatter.3.cloned.1.call-update) | async-done | bytes 524304 | tf_op jit(solution)/shard_map/reduce_scatter | solution.py:55
  108.0 1.7 fusion.31
  109.7 0.8 divide_convert_fusion
  110.5 0.0 all-gather.8.cloned.1.call-update
  110.6 0.0 all-gather.10.cloned.1.call-start
  110.6 27.9 %all-gather.8.cloned.1.call-done = bf16[8,128,1024]{2,1,0:T(8,128)(2,1)} async-done(((bf16[8,16,1024]{2,1,0:T(8,128)(2,1)}), bf16[8,128,1024]{2,1,0:T(8,128)(2,1)}) %all-gather.8.cloned.1.call-update) | async-done | bytes 2097168 | tf_op jit(solution)/shard_map/all_gather | solution.py:57
  138.5 5.1 %fusion.18 = bf16[8,256,128]{1,2,0:T(8,128)(2,1)} fusion(bf16[8,128,1024]{2,1,0:T(8,128)(2,1)} %all-gather.8.cloned.1.call-done, bf16[8,256,1024]{2,1,0:T(8,128)(2,1)} %param.8), kind=kOutput, calls=%fused_computation.21 | convolution fusion | flops 537133056 | bytes 6815744 | tf_op jit(solution)/shard_map/ucl,ukl->ukc/dot_general | solution.py:58
  143.6 0.0 all-gather.10.cloned.1.call-update
  143.7 0.0 all-gather.14.cloned.1.call-start
  143.7 0.5 all-gather.14.cloned.1.call-update
  144.3 0.0 all-gather.12.cloned.1.call-start
  144.3 0.5 all-gather.12.cloned.1.call-update
  144.8 0.0 reduce-scatter.5.cloned.1.call-start
  144.9 1.5 collective-permute-start
  146.4 2.3 collective-permute-start.1
  148.8 24.4 %collective-permute-done = bf16[1024,512]{1,0:T(8,128)(2,1)} collective-permute-done((bf16[1024,512]{1,0:T(8,128)(2,1)}, bf16[1024,512]{1,0:T(8,128)(2,1)}, u32[]{:S(2)}, u32[]{:S(2)}) %collective-permute-start) | collective-permute-done | bytes 1048608 | tf_op jit(solution)/shard_map/ppermute | solution.py:12
  173.1 0.0 collective-permute-start.2
  173.1 8.0 %all-gather.10.cloned.1.call-done = bf16[8,2048,128]{1,2,0:T(8,128)(2,1)} async-done(((bf16[8,256,128]{1,2,0:T(8,128)(2,1)}), bf16[8,2048,128]{1,2,0:T(8,128)(2,1)}) %all-gather.10.cloned.1.call-update) | async-done | bytes 4194320 | tf_op jit(solution)/shard_map/all_gather | solution.py:61
  181.2 3.1 fusion.1
  184.2 101.0 %all-gather.14.cloned.1.call-done = bf16[2048,1024]{1,0:T(8,128)(2,1)} async-done(((bf16[512,1024]{1,0:T(8,128)(2,1)}), bf16[2048,1024]{1,0:T(8,128)(2,1)}) %all-gather.14.cloned.1.call-update) | async-done | bytes 4194320 | tf_op jit(solution)/shard_map/all_gather | solution.py:76
  285.2 9.9 %fusion.4 = f32[8,128,1024]{2,1,0:T(8,128)} fusion(bf16[2048,1024]{1,0:T(8,128)(2,1)} %all-gather.14.cloned.1.call-done, bf16[8,2048,128]{1,2,0:T(8,128)(2,1)} %all-gather.10.cloned.1.call-done, f32[2048]{0:T(1024)S(1)} %copy-done.4, f32[8,128]{1,0:T(8,128)S(1)} %add_rsqrt_fusion), kind=kOutput, calls=%fused_computation.6 | convolution fusion | flops 4303355904 | bytes 12595200 | tf_op jit(solution)/shard_map/ukc,kf->ucf/dot_general | solution.py:73
  295.2 70.3 %all-gather.12.cloned.1.call-done = bf16[2048,1024]{1,0:T(8,128)(2,1)} async-done(((bf16[512,1024]{1,0:T(8,128)(2,1)}), bf16[2048,1024]{1,0:T(8,128)(2,1)}) %all-gather.12.cloned.1.call-update) | async-done | bytes 4194320 | tf_op jit(solution)/shard_map/all_gather | solution.py:70
  365.4 9.6 %multiply_convert_fusion = bf16[8,128,1024]{2,1,0:T(8,128)(2,1)S(1)} fusion(f32[8,128,1024]{2,1,0:T(8,128)} %fusion.4, bf16[2048,1024]{1,0:T(8,128)(2,1)} %all-gather.12.cloned.1.call-done, bf16[8,2048,128]{1,2,0:T(8,128)(2,1)} %all-gather.10.cloned.1.call-done, f32[2048]{0:T(1024)S(1)} %copy-done.4, f32[8,128]{1,0:T(8,128)S(1)} %add_rsqrt_fusion), kind=kOutput, calls=%fused_computation.10 | convolution fusion | flops 4309647360 | bytes 14692352 | tf_op jit(solution)/shard_map/ukc,kf->ucf/dot_general | solution.py:67
  375.1 1.3 copy-done.5
  376.4 2.5 convolution_bitcast_fusion.3
  378.9 0.9 copy.9
  379.7 4.1 convolution_bitcast_fusion.2
  383.8 1.6 copy.10
  385.4 0.0 collective-permute-done.1
  385.4 4.1 convolution_bitcast_fusion.1
  389.5 2.3 copy.11
  391.8 4.1 convolution_bitcast_fusion
  395.9 2.3 copy.12
  398.1 2.5 broadcast_in_dim.26
  400.7 1.2 constant_dynamic-update-slice_fusion.3
  401.8 1.1 constant_dynamic-update-slice_fusion.2
  403.0 1.2 constant_dynamic-update-slice_fusion.1
  404.1 1.2 constant_dynamic-update-slice_fusion
  405.3 0.0 reduce-scatter.5.cloned.1.call-update
  405.3 49.7 %reduce-scatter.5.cloned.1.call-done = bf16[256,8,128]{2,0,1:T(8,128)(2,1)} async-done(((bf16[2048,8,128]{2,0,1:T(8,128)(2,1)}), bf16[256,8,128]{2,0,1:T(8,128)(2,1)}) %reduce-scatter.5.cloned.1.call-update) | async-done | bytes 524304 | tf_op jit(solution)/shard_map/reduce_scatter | solution.py:80
  (13 shorter events, 0.0 us)
Async XLA Ops:
  6.5 42.0 %copy-start = (bf16[256,2048]{1,0:T(8,128)(2,1)S(1)}, bf16[256,2048]{1,0:T(8,128)(2,1)}, u32[]{:S(2)}) copy-start(bf16[256,2048]{1,0:T(8,128)(2,1)} %param.11) | copy-start | bytes 3145732
  6.5 42.0 %all-gather.6.cloned.1.call-start = ((), (), s32[]{:S(2)}) async-start(), calls=%async_computation.2 | async-start | bytes 4718592 | tf_op jit(solution)/shard_map/all_gather | solution.py:46
  7.3 100.8 %reduce-scatter.3.cloned.1.call-start = ((), (), s32[]{:S(2)}) async-start(), calls=%async_computation.3 | async-start | bytes 4718592 | tf_op jit(solution)/shard_map/reduce_scatter | solution.py:55
  56.8 0.7 copy-start.3
  56.8 81.7 %all-gather.8.cloned.1.call-start = ((), (), s32[]{:S(2)}) async-start(), calls=%async_computation.4 | async-start | bytes 2359296 | tf_op jit(solution)/shard_map/all_gather | solution.py:57
  110.6 70.6 %all-gather.10.cloned.1.call-start = ((), (), s32[]{:S(2)}) async-start(), calls=%async_computation.5 | async-start | bytes 4718592 | tf_op jit(solution)/shard_map/all_gather | solution.py:61
  143.6 141.6 %copy-start.4 = (f32[2048]{0:T(1024)S(1)}, f32[2048]{0:T(1024)}, u32[]{:S(2)}) copy-start(f32[2048]{0:T(1024)} %param.12) | copy-start | bytes 24580
  143.7 141.6 %all-gather.14.cloned.1.call-start = ((), (), s32[]{:S(2)}) async-start(), calls=%async_computation.7 | async-start | bytes 5242880 | tf_op jit(solution)/shard_map/all_gather | solution.py:76
  144.3 221.2 %all-gather.12.cloned.1.call-start = ((), (), s32[]{:S(2)}) async-start(), calls=%async_computation.6 | async-start | bytes 5242880 | tf_op jit(solution)/shard_map/all_gather | solution.py:70
  144.8 310.2 %reduce-scatter.5.cloned.1.call-start = ((), (), s32[]{:S(2)}) async-start(), calls=%async_computation.8 | async-start | bytes 4718592 | tf_op jit(solution)/shard_map/reduce_scatter | solution.py:80
  144.9 28.2 %collective-permute-start = (bf16[1024,512]{1,0:T(8,128)(2,1)}, bf16[1024,512]{1,0:T(8,128)(2,1)}, u32[]{:S(2)}, u32[]{:S(2)}) collective-permute-start(bf16[1024,512]{1,0:T(8,128)(2,1)} %param.15), channel_id=1, source_target_pairs={{0,8},{8,16},{16,24},{24,0},{1,9},{9,17},{17,25},{25,1},{2,10},{10... | collective-permute-start | bytes 3145736 | tf_op jit(solution)/shard_map/ppermute | solution.py:12
  146.4 239.0 %collective-permute-start.1 = (bf16[1024,512]{1,0:T(8,128)(2,1)}, bf16[1024,512]{1,0:T(8,128)(2,1)}, u32[]{:S(2)}, u32[]{:S(2)}) collective-permute-start(bf16[1024,512]{1,0:T(8,128)(2,1)} %param.15), channel_id=1, source_target_pairs={{8,0},{16,8},{24,16},{0,24},{9,1},{17,9},{25,17},{1,25},{10,2},{18... | collective-permute-start | bytes 3145736 | tf_op jit(solution)/shard_map/ppermute | solution.py:12
  173.1 218.7 %collective-permute-start.2 = (bf16[1024,512]{1,0:T(8,128)(2,1)}, bf16[1024,512]{1,0:T(8,128)(2,1)}, u32[]{:S(2)}, u32[]{:S(2)}) collective-permute-start(bf16[1024,512]{1,0:T(8,128)(2,1)} %collective-permute-done), channel_id=1, source_target_pairs={{0,8},{8,16},{16,24},{24,0},{1,9},{9,17},{17,25},{25,1},{2,10},{10... | collective-permute-start | bytes 3145736 | tf_op jit(solution)/shard_map/ppermute | solution.py:25
  375.1 1.3 copy-start.5
  398.1 4.8 %copy-start.1 = (bf16[512,8,128]{2,0,1:T(8,128)(2,1)S(1)}, bf16[512,8,128]{2,0,1:T(8,128)(2,1)}, u32[]{:S(2)}) copy-start(bf16[512,8,128]{2,0,1:T(8,128)(2,1)} %copy.11) | copy-start | bytes 3145732
  400.7 3.5 copy-start.2
Sparse Core Ops, SparseCore 0:
  9.2 39.2 all-gather.5
  56.9 51.0 reduce-scatter.2
  110.7 27.7 all-gather.7
  143.8 37.3 all-gather.9
  182.6 102.6 all-gather.13
  286.7 78.7 all-gather.11
  405.4 49.5 reduce-scatter.4
